TPU v7x, 32 devices: a whole 2x2x4 slice. The times are simulated.
32 devices in a mesh: dp: 4 (over y, x), wide: 8 (over z, core).
Axes of the slice: x: 2, y: 2, z: 4, core: 2. Of those that a mesh axis runs over, the one named last changes fastest.
Arguments:
- tokens: bfloat16 [36864, 768], P(('dp', 'wide')), may hold values from -6 to 6
- pos_index: int32 [36864, 2], P(('dp', 'wide')), may hold values from 0 to 196
- size_group: int32 [224], P(('dp', 'wide')), may hold values from 0 to 3, as said below
- pos_table: bfloat16 [197, 768], replicated, may hold values from -3 to 3
- prompts: float32 [50, 768], replicated, may hold values from -6 to 6
- norm_gains: float32 [2, 768], replicated, may hold values from 0.5 to 1.5
- w_qkv: bfloat16 [768, 2304], P('wide'), may hold values from -0.21875 to 0.21875
- w_out: bfloat16 [768, 768], P('wide'), may hold values from -1.75 to 1.75
- w_up: bfloat16 [768, 3072], P('wide'), may hold values from -0.21875 to 0.21875
- w_down: bfloat16 [3072, 768], P('wide'), may hold values from -0.109375 to 0.109375
- cotangent: bfloat16 [36864, 768], P(('dp', 'wide')), may hold values from -6 to 6
Outputs:
- outputs: bfloat16 [36864, 768], P(('dp', 'wide'))
- input_grad: bfloat16 [36864, 768], P(('dp', 'wide'))
- prompt_grad: float32 [50, 768], replicated
- penalty: float32 [], replicated
Inputs may be any that keep to these rules, and one draw needn't show every extreme that they name: `size_group`: 0, 1, 2 name images of 100, 196, 576 patches, 3 an empty slot; the images of one device's 7 slots take at most 1139 of its 1152 rows, and the last device's take exactly that.
All inputs are finite; a program needn't handle non-finite values.
Results may differ from a plain program's by a relative error of at most 0.013.
Values may be sent and summed in bfloat16 or wider, within the bound.
A program may use at most 192 MiB of HBM per device.

v0:
```python
import functools

import jax
import jax.numpy as jnp
from jax import lax
from jax.experimental import pallas as pl
from jax.experimental.pallas import tpu as pltpu
from jax.sharding import PartitionSpec as P

HEADS = 12
HEAD_DIM = 64
PROMPTS = 50
PATCH_S = 100
PATCH_M = 196
PATCH_L = 576

EPSILON = 1e-06
PENALTY_RATE = 3e-05
SCALE = HEAD_DIM**-0.5
LOG2E = 1.4426950408889634
SCORE = SCALE * LOG2E

BF = jnp.bfloat16
F32 = jnp.float32
NN = (((1,), (0,)), ((), ()))
NT = (((1,), (1,)), ((), ()))
MESH = pl.DeviceIdType.MESH

LANES = 128
HEAD_COLS = 384
PAIRS = HEAD_COLS // LANES
GROUP_HEADS = HEAD_COLS // HEAD_DIM
LARGE = 640
KEY_ROWS = (160, 256, LARGE)
QUERY_CHUNKS = (((0, 256),), ((0, 256),), ((0, 256), (256, 256), (512, 128)))
MASKED = -1e30
POS_ROWS = 256
VMEM_LIMIT = 60 << 20
SLOT_ROWS = 64


def dot(a, b, dims=NN):
    return lax.dot_general(a, b, dims, preferred_element_type=F32)


def image_length(group):
    patches = jnp.where(group == 0, PATCH_S, jnp.where(group == 1, PATCH_M, PATCH_L))
    return jnp.where(group == 3, 0, 1 + PROMPTS + patches).astype(jnp.int32)


def total_length(groups, slots):
    total = jnp.int32(0)
    for slot in range(slots):
        total = total + image_length(groups[slot])
    return total


def row_places(groups, slots, first_row, count):
    rows = first_row + lax.broadcasted_iota(jnp.int32, (count, 1), 0)
    place = rows
    start = jnp.int32(0)
    for slot in range(slots):
        length = image_length(groups[slot])
        place = jnp.where((rows >= start) & (length > 0), rows - start, place)
        start = start + length
    live = rows < start
    prompt_slot = jnp.where(live & (place >= 1) & (place <= PROMPTS), place - 1, -1)
    return prompt_slot, live


def norm_parts(values):
    centered = values - jnp.mean(values, axis=-1, keepdims=True)
    rstd = lax.rsqrt(jnp.mean(centered * centered, axis=-1, keepdims=True) + EPSILON)
    return centered * rstd, rstd


def norm_back(normal, rstd, gain, grad):
    scaled = grad * gain
    return (
        scaled
        - jnp.mean(scaled, axis=-1, keepdims=True)
        - normal * jnp.mean(scaled * normal, axis=-1, keepdims=True)
    ) * rstd


def fill_table(table, pos_table, prompts):
    table[...] = jnp.zeros_like(table)
    table[: pos_table.shape[0]] = pos_table[...]
    rest = prompts[...]
    for piece in range(3):
        part = rest.astype(BF)
        first = POS_ROWS + piece * SLOT_ROWS
        table[first : first + PROMPTS] = part
        rest = rest - part.astype(F32)


def embedded(groups, slots, first_row, tokens, pos_index, table):
    prompt_slot, _ = row_places(groups, slots, first_row, tokens.shape[0])
    is_prompt = prompt_slot >= 0
    lane = lax.broadcasted_iota(jnp.int32, (1, POS_ROWS), 1)
    left = jnp.where(is_prompt, -1, pos_index[:, 0:1])
    right = jnp.where(is_prompt, -1, pos_index[:, 1:2])
    half_hot = jnp.where(lane == left, 0.5, 0.0) + jnp.where(lane == right, 0.5, 0.0)
    slot_lane = lax.broadcasted_iota(jnp.int32, (1, 3 * SLOT_ROWS), 1)
    slot_lane = lax.rem(slot_lane, SLOT_ROWS)
    slot_hot = jnp.where(slot_lane == prompt_slot, 1.0, 0.0)
    picked = dot(half_hot.astype(BF), table[:POS_ROWS]) + dot(
        slot_hot.astype(BF), table[POS_ROWS:]
    )
    return jnp.where(is_prompt, 0.0, tokens.astype(F32)) + picked


def embed_kernel(
    slots, groups, tokens, pos_index, pos_table, prompts, gains, w_qkv, hidden_out, qkv_out, table
):
    tile = tokens.shape[0]
    step = pl.program_id(0)

    @pl.when(step == 0)
    def _():
        fill_table(table, pos_table, prompts)

    hidden = embedded(groups, slots, step * tile, tokens[...], pos_index[...], table)
    hidden_out[...] = hidden
    normal, _ = norm_parts(hidden)
    normed = (normal * gains[0:1]).astype(BF)
    qkv_out[...] = dot(normed, w_qkv[...]).astype(BF)


def embed(size_group, tokens, pos_index, pos_table, prompts, gains, w_qkv):
    rows, width = tokens.shape
    tile = 384
    keep = lambda i, g: (0, 0)
    whole = lambda a: pl.BlockSpec(a.shape, keep, pipeline_mode=pl.Buffered(1))
    by_row = lambda columns: pl.BlockSpec((tile, columns), lambda i, g: (i, 0))
    return pl.pallas_call(
        functools.partial(embed_kernel, size_group.shape[0]),
        grid_spec=pltpu.PrefetchScalarGridSpec(
            num_scalar_prefetch=1,
            grid=(rows // tile,),
            in_specs=[
                by_row(width),
                by_row(2),
                whole(pos_table),
                whole(prompts),
                whole(gains),
                whole(w_qkv),
            ],
            out_specs=[by_row(width), by_row(3 * width)],
            scratch_shapes=[pltpu.VMEM((POS_ROWS + 3 * SLOT_ROWS, width), BF)],
        ),
        out_shape=[
            jax.ShapeDtypeStruct((rows, width), F32),
            jax.ShapeDtypeStruct((rows, 3 * width), BF),
        ],
        compiler_params=pltpu.CompilerParams(vmem_limit_bytes=VMEM_LIMIT),
        name="embed",
    )(size_group, tokens, pos_index, pos_table, prompts, gains, w_qkv)


ORDER = (
    ("own", 0, 0), ("own", 0, 1), ("own", 1, 0), ("bring", 0, 0, 0), ("bring", 0, 0, 1),
    ("own", 1, 1), ("embed",), ("pass_on", 0, 0, 0), ("bring", 1, 0, 0), ("bring", 0, 1, 0),
    ("embed",), ("pass_on", 0, 0, 1), ("bring", 0, 1, 1), ("bring", 1, 0, 1),
    ("bring", 0, 2, 0), ("give", 0), ("bring", 0, 2, 1), ("give", 1), ("pass_on", 0, 1, 1),
    ("embed",), ("pass_on", 0, 1, 0), ("bring", 1, 2, 1), ("close", 0, 0), ("bring", 1, 2, 0),
    ("embed",), ("own", 2, 1), ("pass_on", 0, 2, 0), ("pass_on", 0, 2, 1), ("bring", 1, 1, 0),
    ("pass_on", 1, 2, 1), ("own", 2, 0), ("embed",), ("pass_on", 1, 2, 0), ("close", 0, 1),
    ("fetch", 2, 0, 1), ("bring", 1, 1, 1), ("embed",), ("pass_on", 1, 0, 0), ("close", 0, 2),
    ("fetch", 2, 1, 0), ("pass_on", 1, 0, 1), ("fetch", 2, 0, 0), ("all", 0),
    ("pass_on", 1, 1, 0), ("fetch", 2, 1, 1), ("qkv",), ("qkv",), ("pass_on", 1, 1, 1),
    ("qkv",), ("close", 1, 2), ("fetch", 2, 2, 1), ("close", 1, 0), ("qkv",), ("qkv",),
    ("qkv",), ("close", 1, 1), ("fetch", 2, 2, 0), ("all", 1),
)


class Gather:
    def __init__(self, place, index, full, sems, by_rows=False):
        self.dp, self.wide, self.planes, self.plane, self.core = place
        self.index = index
        self.full = full
        self.send, self.recv = sems
        self.rows = full.shape[0] // (2 * self.planes)
        self.columns = full.shape[1] // 8
        self.by_rows = by_rows
        d = self.dp
        self.across = d + 1 - 2 * lax.rem(d, 2)
        self.beyond = lax.rem(d + 2, 4)

    def alpha(self, d):
        return d

    def beta(self, d):
        return 4 + 2 * lax.rem(d, 2) + d // 2

    def pair(self, slot):
        return slot - lax.rem(slot, 2)

    def shard(self, plane, core, slot=None, count=1, array=None):
        full = self.full if array is None else array
        first = pl.multiple_of((2 * plane + core) * self.rows, self.rows)
        if slot is None:
            return full.at[pl.ds(first, self.rows)]
        if self.by_rows:
            step = self.rows // 8
            return full.at[pl.ds(pl.multiple_of(first + slot * step, step), count * step)]
        column = pl.multiple_of(slot * self.columns, self.columns)
        return full.at[pl.ds(first, self.rows), pl.ds(column, count * self.columns)]

    def copy(self, ref, send, recv, device):
        return pltpu.make_async_remote_copy(
            ref,
            ref,
            self.send.at[self.index, send],
            self.recv.at[self.index, recv],
            device_id=device,
            device_id_type=MESH,
        )

    def device(self, plane):
        return (self.dp, 2 * plane + self.core)

    def nearest(self, k):
        n = self.planes
        low = 1 - self.plane // (n // 2)
        edge = low * self.plane + (1 - low) * (n - 1 - self.plane)
        other = k + 1 - (edge - k + n - 1) // n
        return low * other + (1 - low) * (n - 1 - other)

    def along_copies(self, plane, parts=(0, 1)):
        n = self.planes
        up = (plane <= self.plane) & (self.plane < n - 1)
        down = (plane >= self.plane) & (self.plane > 0)
        for part in parts:
            slot = (self.alpha(self.dp), self.beta(self.dp))[part]
            ref = self.shard(plane, self.core, slot)
            sem = 2 * plane + part
            for go, sent, target in (
                (up, sem, lax.rem(self.plane + 1, n)),
                (down, 2 * n + sem, lax.rem(self.plane + n - 1, n)),
            ):
                yield go, self.copy(ref, sent, sem, self.device(target))

    def along(self, plane, parts=(0, 1)):
        for go, copy in self.along_copies(plane, parts):
            pl.when(go)(copy.start)

    def wait_along(self, plane, parts=(0, 1)):
        for part in parts:
            slot = (self.alpha(self.dp), self.beta(self.dp))[part]
            ref = self.shard(plane, self.core, slot)
            sem = 2 * plane + part
            self.copy(ref, sem, sem, self.device(plane)).wait_recv()

    def exchange_copies(self, plane):
        for part, (slot, d) in enumerate(
            ((self.alpha(self.dp), self.across), (self.beta(self.dp), self.beyond))
        ):
            sem = 4 * self.planes + 2 * plane + part
            yield self.copy(self.shard(plane, self.core, slot), sem, sem, (d, self.wide))

    def exchange(self, plane):
        for copy in self.exchange_copies(plane):
            copy.start()

    def wait_one_exchange(self, plane, part):
        d = (self.across, self.beyond)[part]
        slot = (self.alpha, self.beta)[part](d)
        sem = 4 * self.planes + 2 * plane + part
        self.copy(self.shard(plane, self.core, slot), sem, sem, (d, self.wide)).wait_recv()

    def pair_copies(self, plane):
        for part, (slot, d) in enumerate(
            ((self.alpha(self.dp), self.beyond), (self.beta(self.dp), self.across))
        ):
            sem = 6 * self.planes + 2 * plane + part
            ref = self.shard(plane, self.core, self.pair(slot), 2)
            yield self.copy(ref, sem, sem, (d, self.wide))

    def wait_pairs(self, plane):
        for part, (slot, d) in enumerate(
            ((self.alpha(self.beyond), self.beyond), (self.beta(self.across), self.across))
        ):
            sem = 6 * self.planes + 2 * plane + part
            ref = self.shard(plane, self.core, self.pair(slot), 2)
            self.copy(ref, sem, sem, (d, self.wide)).wait_recv()

    def other_core(self):
        return (self.dp, 2 * self.plane + 1 - self.core)

    def give_copy(self, plane):
        sem = 8 * self.planes + plane
        return self.copy(self.shard(plane, self.core), sem, sem, self.other_core())

    def give(self, plane):
        self.give_copy(plane).start()

    def wait_given(self, plane):
        sem = 8 * self.planes + plane
        self.copy(self.shard(plane, 1 - self.core), sem, sem, self.other_core()).wait_recv()

    def wait_all_given(self):
        for plane in range(self.planes):
            self.wait_given(plane)

    def fetch(self, k, part):
        plane = self.nearest(k)
        self.wait_along(plane, (part,))
        self.along(plane, (part,))

    def bring(self, k, part):
        self.fetch(k, part)
        list(self.exchange_copies(self.nearest(k)))[part].start()

    def pass_on(self, k, part):
        plane = self.nearest(k)
        self.wait_one_exchange(plane, part)
        list(self.pair_copies(plane))[part].start()

    def close(self, k):
        plane = self.nearest(k)
        self.wait_pairs(plane)
        self.give(plane)

    def wait_fetched(self):
        for k in range(self.planes):
            plane = self.plane if k == self.planes - 1 else self.nearest(k)
            for go, copy in self.along_copies(plane):
                pl.when(go)(copy.wait_send)

    def wait_passed(self):
        self.give_copy(self.plane).wait_send()
        for k in range(self.planes - 1):
            plane = self.nearest(k)
            for copy in self.exchange_copies(plane):
                copy.wait_send()
            for copy in self.pair_copies(plane):
                copy.wait_send()
            self.give_copy(plane).wait_send()

    def greet(self, planes=True):
        barrier = pltpu.get_barrier_semaphore()
        peers = [(self.across, self.wide), (self.beyond, self.wide), self.other_core()]
        if planes:
            peers += [
                self.device(lax.rem(self.plane + step, self.planes))
                for step in range(1, self.planes)
            ]
        for device in peers:
            pl.semaphore_signal(barrier, inc=1, device_id=device, device_id_type=MESH)
        return barrier, len(peers)

    def fetched(self, k, part, array=None):
        slot = (self.alpha, self.beta)[part](self.dp)
        return self.shard(self.nearest(k), self.core, slot, 1, array)

    @staticmethod
    def semaphores(planes):
        return 9 * planes


def gather_embed_kernel(
    planes,
    slots,
    groups,
    pos_table,
    prompts,
    gains,
    pos_index_t,
    tokens_in,
    own_qkv,
    own_out,
    own_up,
    own_down,
    hidden_out,
    qkv_out,
    full_qkv,
    full_out,
    full_up,
    part_down,
    table,
    tokens,
    pos_index,
    hidden,
    normed,
    qkv,
    first_full,
    second_full,
    third_full,
    send,
    recv,
    local,
):
    d = lax.axis_index("dp")
    w = lax.axis_index("wide")
    place = (d, w, planes, w // 2, lax.rem(w, 2))
    first = Gather(place, 0, first_full, (send, recv))
    second = Gather(place, 1, second_full, (send, recv))
    third = Gather(place, 2, third_full, (send, recv), by_rows=True)
    others = planes - 1
    qkv_columns = own_qkv.shape[1]
    barrier, greeted = first.greet()
    mine = pl.ds(pl.multiple_of(w * first.rows, first.rows), first.rows)
    loads = [
        pltpu.make_async_copy(own_qkv, first_full.at[mine, :qkv_columns], local.at[0]),
        pltpu.make_async_copy(own_out, first_full.at[mine, qkv_columns:], local.at[1]),
        pltpu.make_async_copy(own_up, second_full.at[mine], local.at[2]),
        pltpu.make_async_copy(own_down, third.shard(third.plane, third.core), local.at[3]),
        pltpu.make_async_copy(tokens_in, tokens, local.at[4]),
    ]
    for copy in loads:
        copy.start()
    fill_table(table, pos_table, prompts)
    columns = jnp.concatenate([pos_index_t[...].astype(F32)] * 4, 0).T
    pos_index[...] = columns.astype(jnp.int32)
    for copy in loads[:4]:
        copy.wait()
    pl.semaphore_wait(barrier, greeted)

    rows = tokens.shape[0]
    tiles = ORDER.count(("embed",))
    tile = rows // tiles
    outgoing = []

    def leave(source, target):
        copy = pltpu.make_async_copy(source, target, local.at[7 + len(outgoing)])
        copy.start()
        outgoing.append(copy)

    def embed_tile(index):
        part = slice(index * tile, (index + 1) * tile)
        value = embedded(groups, slots, index * tile, tokens[part], pos_index[part], table)
        hidden[part] = value
        leave(hidden.at[part], hidden_out.at[part])
        normal, _ = norm_parts(value)
        normed[part] = (normal * gains[0:1]).astype(BF)

    def qkv_tile(index):
        part = slice(index * tile, (index + 1) * tile)
        value = normed[part]

        def half(number, done):
            columns = pl.ds(pl.multiple_of(number * qkv_columns // 2, LANES), qkv_columns // 2)
            qkv[part, columns] = dot(value, first_full[:, columns]).astype(BF)
            return done

        lax.fori_loop(0, 2, half, 0)
        leave(qkv.at[part], qkv_out.at[part])

    gathers = (first, second, third)
    embeds, qkvs = iter(range(tiles)), iter(range(tiles))
    leave(second.shard(second.plane, second.core), second.shard(second.plane, second.core, array=full_up))
    for name, *where in ORDER:
        if name == "embed":
            index = next(embeds)
            if index == 0:
                loads[4].wait()
            embed_tile(index)
            continue
        if name == "qkv":
            qkv_tile(next(qkvs))
            continue
        gather, place = gathers[where[0]], where[1:]
        if name == "own":
            gather.along(gather.plane, place)
        elif name == "give":
            gather.give(gather.plane)
        elif name == "bring":
            gather.bring(*place)
        elif name == "fetch":
            gather.fetch(*place)
            leave(gather.fetched(*place), gather.fetched(*place, part_down))
        elif name == "pass_on":
            gather.pass_on(*place)
        elif name == "close":
            gather.close(*place)
            if gather is second:
                plane = second.nearest(*place)
                leave(second.shard(plane, second.core), second.shard(plane, second.core, array=full_up))
        elif gather is first:
            first.wait_all_given()
            leave(first_full.at[:, :qkv_columns], full_qkv)
            leave(first_full.at[:, qkv_columns:], full_out)
        else:
            for k in range(planes):
                plane = second.plane if k == 0 else second.nearest(k - 1)
                second.wait_given(plane)
                core = 1 - second.core
                leave(second.shard(plane, core), second.shard(plane, core, array=full_up))
    first.wait_fetched()
    second.wait_fetched()
    third.wait_fetched()
    first.wait_passed()
    second.wait_passed()
    for copy in outgoing:
        copy.wait()


def can_gather(axes, w_qkv, w_out, w_up, w_down):
    return (
        axes["dp"] == 4
        and axes["wide"] == 8
        and w_qkv.shape[0] % 16 == 0
        and w_down.shape[0] % (8 * 16) == 0
        and w_up.shape[1] % (8 * LANES) == 0
        and (w_qkv.shape[1] + w_out.shape[1]) % (8 * LANES) == 0
    )


def gather_embed(
    axes, size_group, tokens, pos_index, pos_table, prompts, gains, w_qkv, w_out, w_up, w_down
):
    rows, width = tokens.shape
    wide = axes["wide"]
    planes = wide // 2
    depth = w_qkv.shape[0] * wide
    inner_width = w_up.shape[1]
    vmem = pl.BlockSpec(memory_space=pltpu.VMEM)
    hbm = pl.BlockSpec(memory_space=pltpu.HBM)
    dma = pltpu.SemaphoreType.DMA
    count = Gather.semaphores(planes)
    first_columns = w_qkv.shape[1] + w_out.shape[1]
    return pl.pallas_call(
        functools.partial(gather_embed_kernel, planes, size_group.shape[0]),
        in_specs=[pl.BlockSpec(memory_space=pltpu.SMEM)] + [vmem] * 4 + [hbm] * 5,
        out_specs=[hbm] * 6,
        out_shape=[
            jax.ShapeDtypeStruct((rows, width), F32),
            jax.ShapeDtypeStruct((rows, w_qkv.shape[1]), BF),
            jax.ShapeDtypeStruct((depth, w_qkv.shape[1]), BF),
            jax.ShapeDtypeStruct((depth, w_out.shape[1]), BF),
            jax.ShapeDtypeStruct((depth, inner_width), BF),
            jax.ShapeDtypeStruct((inner_width, width), BF),
        ],
        scratch_shapes=[
            pltpu.VMEM((POS_ROWS + 3 * SLOT_ROWS, width), BF),
            pltpu.VMEM((rows, width), BF),
            pltpu.VMEM((rows, 8), jnp.int32),
            pltpu.VMEM((rows, width), F32),
            pltpu.VMEM((rows, width), BF),
            pltpu.VMEM((rows, w_qkv.shape[1]), BF),
            pltpu.VMEM((depth, first_columns), BF),
            pltpu.VMEM((depth, inner_width), BF),
            pltpu.VMEM((inner_width, width), BF),
            dma((3, count)),
            dma((3, count)),
            dma((7 + 2 * ORDER.count(("embed",)) + 2 + 2 * planes + 2 * (planes - 1),)),
        ],
        compiler_params=pltpu.CompilerParams(
            collective_id=0, has_side_effects=True, vmem_limit_bytes=VMEM_LIMIT
        ),
        name="gather_embed",
    )(
        size_group, pos_table, prompts, gains, pos_index.T, tokens, w_qkv, w_out, w_up, w_down
    )


def each_image(groups, slots, image):
    def body(slot, start):
        group = groups[slot]
        length = image_length(group)
        for size in range(3):
            pl.when(group == size)(functools.partial(image, size, start, length, slot))
        return start + length

    lax.fori_loop(0, slots, body, jnp.int32(0))


def window(count, rows, start, length):
    first = jnp.minimum((start // 8) * 8, rows - count)
    return pl.multiple_of(first, 8), start - first


def in_image(count, shift, length, first=0):
    row = lax.broadcasted_iota(jnp.int32, (count, LANES), 0) + first
    return (row >= shift) & (row < shift + length)


def head_lanes(head):
    lane = lax.broadcasted_iota(jnp.int32, (1, LANES), 1)
    return (lane < HEAD_DIM) if head % 2 == 0 else (lane >= HEAD_DIM)


def one_head(values, head, other):
    return jnp.where(head_lanes(head), values, other)


def marker(head):
    lane = lax.broadcasted_iota(jnp.int32, (1, LANES), 1)
    return jnp.where(lane == HEAD_DIM * (1 - head % 2), 1.0, 0.0).astype(BF)


def take(ref, rows):
    return [ref[rows, LANES * pair : LANES * (pair + 1)] for pair in range(PAIRS)]


def put(ref, rows, pair, new, inside):
    columns = slice(LANES * pair, LANES * (pair + 1))
    old = ref[rows, columns].astype(F32)
    ref[rows, columns] = jnp.where(inside, new, old).astype(BF)


def low(parts):
    return [part.astype(BF) for part in parts]


def head_rows(values, head):
    return values[HEAD_DIM * (head % 2) : HEAD_DIM * (head % 2 + 1)]


def own_quarters(values):
    count = values.shape[1] // 2
    return [values[:HEAD_DIM, :count], values[HEAD_DIM : 2 * HEAD_DIM, count:]]


def blocks_of(count):
    if count == LANES:
        return [(2 * pair, 2 * pair + 1) for pair in range(PAIRS)]
    return [(head,) for head in range(GROUP_HEADS)]


class Keys:
    def __init__(self, ref, rows, inside):
        self.pairs = take(ref, rows)
        bias = jnp.where(inside, 0.0, MASKED)
        self.bias = jnp.concatenate([bias, bias], 1)
        low_bias = bias.astype(BF)
        self.heads = [one_head(self.pairs[h // 2], h, low_bias) for h in range(GROUP_HEADS)]

    def scores(self, block, queries):
        if len(block) == 1:
            head = block[0]
            return dot(self.heads[head], one_head(queries[head // 2], head, marker(head)), NT)
        return dot(self.pairs[block[0] // 2], stacked(block, queries), NT) + self.bias


def stacked(block, parts):
    zero = jnp.zeros((1, LANES), BF)
    return jnp.concatenate([one_head(parts[h // 2], h, zero) for h in block], 0)


def attend_kernel(slots, groups, q_ref, k_ref, v_ref, out_ref, total_ref):
    out_ref[...] = jnp.zeros_like(out_ref)

    def image(size, start, length, slot):
        all_rows = out_ref.shape[0]
        span = KEY_ROWS[size]
        chunks = QUERY_CHUNKS[size]
        key_first, key_shift = window(span, all_rows, start, length)
        first, shift = window(max(span, 256), all_rows, start, length)
        key_rows = pl.ds(key_first, span)
        keys = Keys(k_ref, key_rows, in_image(span, key_shift, length))
        ones = jnp.ones((8, span), BF)
        value_t = [x.T for x in take(v_ref, key_rows)]

        def values_of(block):
            pair = value_t[block[0] // 2]
            rows = pair if len(block) == 2 else head_rows(pair, block[0])
            return jnp.concatenate([rows, ones], 0)

        for chunk, count in chunks:
            rows = pl.ds(pl.multiple_of(first + chunk, 8), count)
            query = take(q_ref, rows)
            blocks = blocks_of(count)
            scores = [keys.scores(block, query) for block in blocks]
            peaks = [jnp.max(s, axis=0, keepdims=True) * SCORE for s in scores]
            powers = [jnp.exp2(s * SCORE - m).astype(BF) for s, m in zip(scores, peaks)]
            mixed = [dot(values_of(block), e) for block, e in zip(blocks, powers)]
            parts = []
            for block, peak, value in zip(blocks, peaks, mixed):
                depth = HEAD_DIM * len(block)
                sums = value[depth : depth + 1]
                total = peak + jnp.log2(sums)
                for number, head in enumerate(block):
                    total_ref[0, GROUP_HEADS * slot + head, :, chunk : chunk + count] = total[
                        :, number * count : (number + 1) * count
                    ]
                value = value[:depth] / sums
                parts += [value] if len(block) == 1 else own_quarters(value)
            inside = in_image(count, shift, length, chunk)
            for pair in range(PAIRS):
                put(out_ref, rows, pair, jnp.concatenate(parts[2 * pair : 2 * pair + 2], 0).T, inside)

    each_image(groups, slots, image)


def attend(size_group, qkv):
    rows = qkv.shape[0]
    width = qkv.shape[1] // 3
    steps = width // HEAD_COLS
    slots = size_group.shape[0]
    block = lambda shift: pl.BlockSpec((rows, HEAD_COLS), lambda i, g: (0, shift * steps + i))
    return pl.pallas_call(
        functools.partial(attend_kernel, slots),
        grid_spec=pltpu.PrefetchScalarGridSpec(
            num_scalar_prefetch=1,
            grid=(steps,),
            in_specs=[block(0), block(1), block(2)],
            out_specs=[
                block(0),
                pl.BlockSpec((1, GROUP_HEADS * slots, 1, LARGE), lambda i, g: (i, 0, 0, 0)),
            ],
        ),
        out_shape=[
            jax.ShapeDtypeStruct((rows, width), BF),
            jax.ShapeDtypeStruct((steps, GROUP_HEADS * slots, 1, LARGE), F32),
        ],
        compiler_params=pltpu.CompilerParams(vmem_limit_bytes=VMEM_LIMIT),
        name="attend",
    )(size_group, qkv, qkv, qkv)


def attend_back_kernel(slots, groups, q_ref, k_ref, v_ref, grad_ref, mixed_ref, total_ref, *refs):
    middles, refs = refs[:PAIRS], refs[PAIRS:]
    passed_in, dq_ref, dk_ref, dv_ref, dq_sum, dk_sum, dv_sum, middle_sum, passed_out = refs
    passed_out[...] = passed_in[...]
    for ref in (dq_sum, dk_sum, dv_sum, middle_sum):
        ref[...] = jnp.zeros_like(ref)

    def image(size, start, length, slot):
        all_rows = dq_ref.shape[0]
        span = KEY_ROWS[size]
        chunks = QUERY_CHUNKS[size]
        key_first, key_shift = window(span, all_rows, start, length)
        first, shift = window(max(span, 256), all_rows, start, length)
        key_rows = pl.ds(key_first, span)
        key_inside = in_image(span, key_shift, length)
        keys = Keys(k_ref, key_rows, key_inside)
        key_t = [x.T for x in keys.pairs]
        value = take(v_ref, key_rows)
        dk = [jnp.zeros((span, LANES), F32)] * PAIRS
        dv = [jnp.zeros((span, LANES), F32)] * PAIRS

        def add_prompts(total, pair, values, before):
            count = min(values.shape[0], 256)
            slot_row = lax.broadcasted_iota(jnp.int32, (SLOT_ROWS, count), 0)
            row = lax.broadcasted_iota(jnp.int32, (SLOT_ROWS, count), 1)
            chosen = (row == slot_row + before + 1) & (slot_row < PROMPTS)
            chosen = jnp.where(chosen, 1.0, 0.0).astype(BF)
            columns = slice(LANES * pair, LANES * (pair + 1))
            total[:, columns] += dot(chosen, values[:count].astype(BF))

        for chunk, count in chunks:
            rows = pl.ds(pl.multiple_of(first + chunk, 8), count)
            inside = in_image(count, shift, length, chunk)
            query = take(q_ref, rows)
            grad32 = [jnp.where(inside, x.astype(F32), 0.0) for x in take(grad_ref, rows)]
            products = [(x * y.astype(F32)).T for x, y in zip(grad32, take(mixed_ref, rows))]
            grad = low(grad32)
            blocks = blocks_of(count)
            queries = [stacked(block, query) for block in blocks]
            grads = [stacked(block, grad) for block in blocks]
            scores = [keys.scores(block, query) for block in blocks]
            prob_grads = [dot(value[block[0] // 2], g, NT) for block, g in zip(blocks, grads)]

            def side_by_side(block, row_of):
                found = [row_of(head) for head in block]
                return found[0] if len(found) == 1 else jnp.concatenate(found, 1)

            totals = [
                side_by_side(
                    block, lambda h: total_ref[0, GROUP_HEADS * slot + h, :, chunk : chunk + count]
                )
                for block in blocks
            ]
            deltas = [
                side_by_side(
                    block,
                    lambda h: jnp.sum(head_rows(products[h // 2], h), axis=0, keepdims=True),
                )
                for block in blocks
            ]
            probs = [jnp.exp2(s * SCORE - t) for s, t in zip(scores, totals)]
            score_grads = [
                (p * (g - t)).astype(BF) for p, g, t in zip(probs, prob_grads, deltas)
            ]
            parts = []
            for block, prob, score_grad, q, g in zip(blocks, probs, score_grads, queries, grads):
                pair = block[0] // 2
                dv[pair] += dot(prob.astype(BF), g)
                dk[pair] += dot(score_grad, q)
                if len(block) == 1:
                    parts.append(dot(head_rows(key_t[pair], block[0]), score_grad))
                else:
                    parts += own_quarters(dot(key_t[pair], score_grad))
            for pair in range(PAIRS):
                dq = jnp.concatenate(parts[2 * pair : 2 * pair + 2], 0).T * SCALE
                put(dq_ref, rows, pair, dq, inside)
                if chunk == 0:
                    add_prompts(dq_sum, pair, dq, shift)
        for pair in range(PAIRS):
            put(dk_ref, key_rows, pair, dk[pair] * SCALE, key_inside)
            put(dv_ref, key_rows, pair, dv[pair], key_inside)
            add_prompts(dk_sum, pair, dk[pair] * SCALE, key_shift)
            add_prompts(dv_sum, pair, dv[pair], key_shift)
            columns = slice(LANES * pair, LANES * (pair + 1))
            middle_sum[:, columns] += middles[pair][pl.ds(start + 1, SLOT_ROWS), :]

    each_image(groups, slots, image)


def attend_back(size_group, qkv, mixed_grad, mixed, totals, middle_grad, passed):
    rows = qkv.shape[0]
    width = qkv.shape[1] // 3
    steps = width // HEAD_COLS
    slots = size_group.shape[0]
    block = lambda shift: pl.BlockSpec((rows, HEAD_COLS), lambda i, g: (0, shift * steps + i))
    middle = lambda pair: pl.BlockSpec((rows, LANES), lambda i, g: (0, PAIRS * i + pair))
    return pl.pallas_call(
        functools.partial(attend_back_kernel, slots),
        grid_spec=pltpu.PrefetchScalarGridSpec(
            num_scalar_prefetch=1,
            grid=(steps,),
            in_specs=[
                block(0),
                block(1),
                block(2),
                block(0),
                block(0),
                pl.BlockSpec((1, GROUP_HEADS * slots, 1, LARGE), lambda i, g: (i, 0, 0, 0)),
            ]
            + [middle(pair) for pair in range(PAIRS)]
            + [block(0)],
            out_specs=[block(0)] * 3
            + [pl.BlockSpec((SLOT_ROWS, HEAD_COLS), lambda i, g: (0, i))] * 4
            + [block(0)],
        ),
        out_shape=[jax.ShapeDtypeStruct((rows, width), BF)] * 3
        + [jax.ShapeDtypeStruct((SLOT_ROWS, width), F32)] * 4
        + [jax.ShapeDtypeStruct((rows, width), BF)],
        compiler_params=pltpu.CompilerParams(vmem_limit_bytes=VMEM_LIMIT),
        name="attend_back",
    )(
        size_group,
        qkv,
        qkv,
        qkv,
        mixed_grad,
        mixed,
        totals,
        *[middle_grad] * PAIRS,
        passed,
    )


def feed_kernel(
    slots,
    chunk,
    groups,
    hidden,
    mixed,
    cotangent,
    gains,
    w_out,
    w_up,
    w_down,
    out_ref,
    middle_grad_ref,
    mixed_grad_ref,
):
    tile = hidden.shape[0]
    inner_width = w_up.shape[1]
    rows = pl.program_id(0) * tile + lax.broadcasted_iota(jnp.int32, (tile, 1), 0)
    live = rows < total_length(groups, slots)
    out_grad = jnp.where(live, cotangent[...].astype(F32), 0.0)
    out_grad_low = out_grad.astype(BF)
    middle = hidden[...] + dot(mixed[...], w_out[...])
    normal, rstd = norm_parts(middle)
    gain = gains[1:2]
    second = (normal * gain).astype(BF)
    forward = middle
    back = jnp.zeros_like(middle)
    for first in range(0, inner_width, chunk):
        part = slice(first, first + chunk)
        inner = dot(second, w_up[:, part])
        act_grad = dot(out_grad_low, w_down[part], NT)
        phi = 0.5 + 0.5 * lax.erf(inner * (0.5**0.5))
        density = jnp.exp2(inner * inner * (-0.5 * LOG2E)) * 0.3989422804014327
        activated = (inner * phi).astype(BF)
        inner_grad = (act_grad * (phi + inner * density)).astype(BF)
        forward = forward + dot(activated, w_down[part])
        back = back + dot(inner_grad, w_up[:, part], NT)
    out_ref[...] = jnp.where(live, forward, 0.0).astype(BF)
    middle_grad = out_grad + norm_back(normal, rstd, gain, back)
    middle_grad_ref[...] = middle_grad
    mixed_grad_ref[...] = dot(middle_grad.astype(BF), w_out[...], NT).astype(BF)


def feed(size_group, hidden, mixed, cotangent, gains, w_out, w_up, w_down):
    rows, width = hidden.shape
    tile = 384
    chunk = 512
    keep = lambda i, g: (0, 0)
    whole = lambda a: pl.BlockSpec(a.shape, keep, pipeline_mode=pl.Buffered(1))
    by_row = pl.BlockSpec((tile, width), lambda i, g: (i, 0))
    return pl.pallas_call(
        functools.partial(feed_kernel, size_group.shape[0], chunk),
        grid_spec=pltpu.PrefetchScalarGridSpec(
            num_scalar_prefetch=1,
            grid=(rows // tile,),
            in_specs=[by_row, by_row, by_row, whole(gains), whole(w_out), whole(w_up), whole(w_down)],
            out_specs=[by_row, by_row, by_row],
        ),
        out_shape=[
            jax.ShapeDtypeStruct((rows, width), BF),
            jax.ShapeDtypeStruct((rows, width), F32),
            jax.ShapeDtypeStruct((rows, width), BF),
        ],
        compiler_params=pltpu.CompilerParams(vmem_limit_bytes=VMEM_LIMIT),
        name="feed",
    )(size_group, hidden, mixed, cotangent, gains, w_out, w_up, w_down)


def gather_feed_kernel(
    planes,
    slots,
    chunk,
    groups,
    gains,
    hidden_in,
    mixed_in,
    cotangent_in,
    full_out,
    full_up,
    own_down,
    part_down,
    out_ref,
    middle_grad_ref,
    mixed_grad_ref,
    middle,
    mixed,
    cotangent,
    w_out,
    w_up,
    w_down,
    active,
    slope,
    send,
    recv,
    weights_in,
    rows_in,
    rows_out,
):
    d = lax.axis_index("dp")
    w = lax.axis_index("wide")
    down = Gather((d, w, planes, w // 2, lax.rem(w, 2)), 0, w_down, (send, recv), by_rows=True)
    barrier, greeted = down.greet(planes=False)
    others = planes - 1
    tiles = rows_in.shape[0]
    tile = middle.shape[0] // tiles
    inner_width = w_up.shape[1]

    def tile_rows(index):
        return pl.ds(pl.multiple_of(index * tile, tile), tile)

    def loads(index):
        part = tile_rows(index)
        return [
            pltpu.make_async_copy(hidden_in.at[part], middle.at[part], rows_in.at[index, 0]),
            pltpu.make_async_copy(mixed_in.at[part], mixed.at[part], rows_in.at[index, 1]),
            pltpu.make_async_copy(cotangent_in.at[part], cotangent.at[part], rows_in.at[index, 2]),
        ]

    def stores(index):
        part = tile_rows(index)
        return [
            pltpu.make_async_copy(middle.at[part], middle_grad_ref.at[part], rows_out.at[index, 0]),
            pltpu.make_async_copy(mixed.at[part], mixed_grad_ref.at[part], rows_out.at[index, 1]),
            pltpu.make_async_copy(cotangent.at[part], out_ref.at[part], rows_out.at[index, 2]),
        ]

    down_loads = [(own_down, down.shard(down.plane, down.core))]
    for k in range(others):
        for part in (0, 1):
            down_loads.append((down.fetched(k, part, part_down), down.fetched(k, part)))
    down_loads = [
        pltpu.make_async_copy(source, target, weights_in.at[2 + index])
        for index, (source, target) in enumerate(down_loads)
    ]
    out_load = pltpu.make_async_copy(full_out, w_out, weights_in.at[0])
    up_load = pltpu.make_async_copy(full_up, w_up, weights_in.at[1])
    for copy in down_loads:
        copy.start()
    out_load.start()
    for copy in loads(0):
        copy.start()
    up_load.start()
    for index in range(1, tiles):
        for copy in loads(index):
            copy.start()
    for copy in down_loads:
        copy.wait()
    pl.semaphore_wait(barrier, greeted)
    for k in range(others):
        down.exchange(down.nearest(k))
    down.give(down.plane)
    out_load.wait()
    up_load.wait()
    gain = gains[1:2]

    def pump(step):
        @pl.when((step >= 0) & (step < others))
        def _():
            down.pass_on(step, 0)
            down.pass_on(step, 1)

        @pl.when((step >= 2) & (step < others + 2))
        def _():
            down.close(step - 2)

    def up_tile(index, carry):
        for copy in loads(index):
            copy.wait()
        part = tile_rows(index)
        value = middle[part, :] + dot(mixed[part, :], w_out[...])
        middle[part, :] = value
        normal, _ = norm_parts(value)
        second = (normal * gain).astype(BF)
        for first in range(0, inner_width, chunk):
            columns = slice(first, first + chunk)
            inner = dot(second, w_up[:, columns])
            phi = 0.5 + 0.5 * lax.erf(inner * (0.5**0.5))
            density = jnp.exp2(inner * inner * (-0.5 * LOG2E)) * 0.3989422804014327
            active[part, columns] = (inner * phi).astype(BF)
            slope[part, columns] = phi + inner * density
            if first + chunk == inner_width // 2:
                pump(2 * index)
        pump(2 * index + 1)
        return carry

    lax.fori_loop(0, tiles, up_tile, 0)
    for step in range(2 * tiles, others + 2):
        pump(step)
    down.wait_all_given()
    total = total_length(groups, slots)

    def down_tile(index, carry):
        part = tile_rows(index)
        rows = index * tile + lax.broadcasted_iota(jnp.int32, (tile, 1), 0)
        live = rows < total
        out_grad = jnp.where(live, cotangent[part, :].astype(F32), 0.0)
        out_grad_low = out_grad.astype(BF)
        value = middle[part, :]
        back = jnp.zeros_like(value)
        for first in range(0, inner_width, chunk):
            columns = slice(first, first + chunk)
            act_grad = dot(out_grad_low, w_down[columns], NT)
            inner_grad = (act_grad * slope[part, columns]).astype(BF)
            back = back + dot(inner_grad, w_up[:, columns], NT)
        forward = value + dot(active[part, :], w_down[...])
        cotangent[part, :] = jnp.where(live, forward, 0.0).astype(BF)
        normal, rstd = norm_parts(value)
        middle_grad = out_grad + norm_back(normal, rstd, gain, back)
        middle[part, :] = middle_grad
        mixed[part, :] = dot(middle_grad.astype(BF), w_out[...], NT).astype(BF)
        for copy in stores(index):
            copy.start()
        return carry

    lax.fori_loop(0, tiles, down_tile, 0)
    down.wait_passed()
    for index in range(tiles):
        for copy in stores(index):
            copy.wait()


def gather_feed(axes, size_group, hidden, mixed, cotangent, gains, w_out, w_up, w_down, part_down):
    rows, width = hidden.shape
    planes = axes["wide"] // 2
    inner_width = w_up.shape[1]
    tiles = 3
    hbm = pl.BlockSpec(memory_space=pltpu.HBM)
    dma = pltpu.SemaphoreType.DMA
    count = Gather.semaphores(planes)
    return pl.pallas_call(
        functools.partial(gather_feed_kernel, planes, size_group.shape[0], 512),
        in_specs=[
            pl.BlockSpec(memory_space=pltpu.SMEM),
            pl.BlockSpec(memory_space=pltpu.VMEM),
        ]
        + [hbm] * 7,
        out_specs=[hbm] * 3,
        out_shape=[
            jax.ShapeDtypeStruct((rows, width), BF),
            jax.ShapeDtypeStruct((rows, width), F32),
            jax.ShapeDtypeStruct((rows, width), BF),
        ],
        scratch_shapes=[
            pltpu.VMEM((rows, width), F32),
            pltpu.VMEM((rows, width), BF),
            pltpu.VMEM((rows, width), BF),
            pltpu.VMEM(w_out.shape, BF),
            pltpu.VMEM(w_up.shape, BF),
            pltpu.VMEM((inner_width, width), BF),
            pltpu.VMEM((rows, inner_width), BF),
            pltpu.VMEM((rows, inner_width), F32),
            dma((1, count)),
            dma((1, count)),
            dma((3 + 2 * (planes - 1),)),
            dma((tiles, 3)),
            dma((tiles, 3)),
        ],
        compiler_params=pltpu.CompilerParams(
            collective_id=2, has_side_effects=True, vmem_limit_bytes=VMEM_LIMIT
        ),
        name="gather_feed",
    )(size_group, gains, hidden, mixed, cotangent, w_out, w_up, w_down, part_down)


class Shared:
    def __init__(self, dp, wide, mine, near, far, result, sems):
        self.members = 2 * dp
        self.planes = wide // 2
        self.rows = mine.shape[0] // self.members
        self.d = lax.axis_index("dp")
        w = lax.axis_index("wide")
        self.plane = w // 2
        self.core = lax.rem(w, 2)
        self.member = self.d * 2 + self.core
        self.mine, self.near, self.far, self.result = mine, near, far, result
        self.send, self.near_in, self.far_in, self.last_in = sems

    def peer(self, step):
        other = lax.rem(self.member + step, self.members)
        return other, (other // 2, self.plane * 2 + lax.rem(other, 2))

    def plane_peer(self, step):
        other = lax.rem(self.plane + step, self.planes)
        return other, (self.d, other * 2 + self.core)

    def greet(self):
        barrier = pltpu.get_barrier_semaphore()
        for step in range(1, self.members):
            pl.semaphore_signal(barrier, inc=1, device_id=self.peer(step)[1], device_id_type=MESH)
        for step in range(1, self.planes):
            pl.semaphore_signal(
                barrier, inc=1, device_id=self.plane_peer(step)[1], device_id_type=MESH
            )
        return barrier, self.members + self.planes - 2

    def part(self, ref, index):
        return ref.at[pl.ds(pl.multiple_of(index * self.rows, self.rows), self.rows)]

    def copy(self, source, target, send, recv, device):
        return pltpu.make_async_remote_copy(
            source, target, send, recv, device_id=device, device_id_type=MESH
        )

    def first(self, step):
        other, device = self.peer(step)
        return self.copy(
            self.part(self.mine, other),
            self.near.at[step],
            self.send.at[0, step],
            self.near_in.at[step],
            device,
        )

    def second(self, step):
        mine = self.far.at[self.plane]
        device = self.plane_peer(step)[1]
        return self.copy(mine, mine, self.send.at[1, step], self.far_in.at[step], device)

    def third(self, step):
        mine = self.part(self.result, self.member)
        device = self.peer(step)[1]
        return self.copy(mine, mine, self.send.at[2, step], self.last_in.at[step], device)

    def start_first(self):
        for step in range(1, self.members):
            self.first(step).start()
        self.near[0] = self.part(self.mine, self.member)[...]

    def start_second(self):
        for step in range(1, self.members):
            self.first(step).wait_recv()
        total = jnp.zeros(self.near.shape[1:], F32)
        for index in range(self.members):
            total = total + self.near[lax.rem(self.member - index + self.members, self.members)]
        self.far[self.plane] = total
        for step in range(1, self.planes):
            self.second(step).start()

    def start_third(self):
        for step in range(1, self.planes):
            self.second(step).wait_recv()
        total = jnp.zeros(self.near.shape[1:], F32)
        for index in range(self.planes):
            total = total + self.far[index]
        self.part(self.result, self.member)[...] = total
        for step in range(1, self.members):
            self.third(step).start()

    def end(self):
        for step in range(1, self.members):
            self.third(step).wait_recv()
        for step in range(1, self.members):
            self.first(step).wait_send()
            self.third(step).wait_send()
        for step in range(1, self.planes):
            self.second(step).wait_send()


def finish_kernel(
    dp,
    wide,
    slots,
    groups,
    prompts,
    gains,
    dq_sum,
    dk_sum,
    dv_sum,
    middle_sum,
    hidden_in,
    middle_grad_in,
    dq_in,
    dk_in,
    dv_in,
    w_qkv_in,
    input_grad_out,
    prompt_grad,
    penalty,
    hidden,
    middle_grad,
    dq,
    dk,
    dv,
    w_qkv,
    input_grad,
    known,
    mine,
    near,
    far,
    result,
    send,
    near_in,
    far_in,
    last_in,
    weight_in,
    rows_in,
    rows_out,
):
    shared = Shared(dp, wide, mine, near, far, result, (send, near_in, far_in, last_in))
    barrier, greeted = shared.greet()
    tiles = rows_in.shape[0]
    width = hidden.shape[1]
    tile = hidden.shape[0] // tiles
    weight_load = pltpu.make_async_copy(w_qkv_in, w_qkv, weight_in)
    weight_load.start()

    def tile_rows(index):
        return pl.ds(pl.multiple_of(index * tile, tile), tile)

    def loads(index):
        part = tile_rows(index)
        pairs = (
            (dq_in, dq),
            (dk_in, dk),
            (dv_in, dv),
            (hidden_in, hidden),
            (middle_grad_in, middle_grad),
        )
        return [
            pltpu.make_async_copy(source.at[part], target.at[part], rows_in.at[index, number])
            for number, (source, target) in enumerate(pairs)
        ]

    for index in range(tiles):
        for copy in loads(index):
            copy.start()

    def back(q, k, v):
        return (
            dot(q, w_qkv[:, :width], NT)
            + dot(k, w_qkv[:, width : 2 * width], NT)
            + dot(v, w_qkv[:, 2 * width :], NT)
        )

    known[...] = jnp.zeros_like(known)
    known[: prompts.shape[0]] = prompts[...]
    pieces = []
    for ref in (dq_sum, dk_sum, dv_sum):
        rest = ref[...]
        terms = []
        for _ in range(2):
            terms.append(rest.astype(BF))
            rest = rest - terms[-1].astype(F32)
        pieces.append(jnp.concatenate(terms, 0))
    weight_load.wait()
    terms = back(*pieces)
    normed_grad = terms[:SLOT_ROWS] + terms[SLOT_ROWS:]
    normal, rstd = norm_parts(known[...])
    local = middle_sum[...] + norm_back(normal, rstd, gains[0:1], normed_grad)
    slot_row = lax.broadcasted_iota(jnp.int32, (SLOT_ROWS, 1), 0)
    count = total_length(groups, slots).astype(F32)
    mine[...] = jnp.where(slot_row < PROMPTS, local, jnp.where(slot_row == PROMPTS, count, 0.0))
    pl.semaphore_wait(barrier, greeted)
    shared.start_first()

    def store(index):
        part = tile_rows(index)
        return pltpu.make_async_copy(
            input_grad.at[part], input_grad_out.at[part], rows_out.at[index]
        )

    def row_tile(index, carry):
        for copy in loads(index):
            copy.wait()
        part = tile_rows(index)
        normal, rstd = norm_parts(hidden[part, :])
        normed_grad = back(dq[part, :], dk[part, :], dv[part, :])
        hidden_grad = middle_grad[part, :] + norm_back(normal, rstd, gains[0:1], normed_grad)
        prompt_slot, live = row_places(groups, slots, index * tile, tile)
        input_grad[part, :] = jnp.where(live & (prompt_slot < 0), hidden_grad, 0.0).astype(BF)
        store(index).start()
        pl.when(index == 0)(shared.start_second)
        pl.when(index == 1)(shared.start_third)
        return carry

    lax.fori_loop(0, tiles, row_tile, 0)
    shared.end()
    given = prompts[...]
    size = given.shape[0] * given.shape[1]
    count = result[PROMPTS : PROMPTS + 1]
    prompt_grad[...] = result[:PROMPTS] + (2.0 * PENALTY_RATE / size) * count * given
    square = jnp.sum(jnp.sum(given * given, axis=1, keepdims=True), axis=0, keepdims=True)
    penalty[...] = PENALTY_RATE * count[:, :1] * (square / size)
    for index in range(tiles):
        store(index).wait()


def finish(axes, size_group, prompts, gains, sums, hidden, middle_grad, dq, dk, dv, w_qkv):
    rows, width = hidden.shape
    dp, wide = axes["dp"], axes["wide"]
    members, planes = 2 * dp, wide // 2
    tiles = 3
    dma = pltpu.SemaphoreType.DMA
    vmem = pl.BlockSpec(memory_space=pltpu.VMEM)
    hbm = pl.BlockSpec(memory_space=pltpu.HBM)
    input_grad, prompt_grad, penalty = pl.pallas_call(
        functools.partial(finish_kernel, dp, wide, size_group.shape[0]),
        in_specs=[pl.BlockSpec(memory_space=pltpu.SMEM)] + [vmem] * 6 + [hbm] * 6,
        out_specs=[hbm, vmem, vmem],
        out_shape=[
            jax.ShapeDtypeStruct((rows, width), BF),
            jax.ShapeDtypeStruct(prompts.shape, F32),
            jax.ShapeDtypeStruct((1, 1), F32),
        ],
        scratch_shapes=[
            pltpu.VMEM((rows, width), F32),
            pltpu.VMEM((rows, width), F32),
            pltpu.VMEM((rows, width), BF),
            pltpu.VMEM((rows, width), BF),
            pltpu.VMEM((rows, width), BF),
            pltpu.VMEM(w_qkv.shape, BF),
            pltpu.VMEM((rows, width), BF),
            pltpu.VMEM((SLOT_ROWS, width), F32),
            pltpu.VMEM((SLOT_ROWS, width), F32),
            pltpu.VMEM((members, SLOT_ROWS // members, width), F32),
            pltpu.VMEM((planes, SLOT_ROWS // members, width), F32),
            pltpu.VMEM((SLOT_ROWS, width), F32),
            dma((3, max(members, planes))),
            dma((members,)),
            dma((planes,)),
            dma((members,)),
            dma,
            dma((tiles, 5)),
            dma((tiles,)),
        ],
        compiler_params=pltpu.CompilerParams(
            collective_id=1, has_side_effects=True, vmem_limit_bytes=VMEM_LIMIT
        ),
        name="finish",
    )(size_group, prompts, gains, *sums, hidden, middle_grad, dq, dk, dv, w_qkv)
    return input_grad, prompt_grad, penalty[0, 0]


def shards(
    axes,
    tokens,
    pos_index,
    size_group,
    pos_table,
    prompts,
    norm_gains,
    w_qkv,
    w_out,
    w_up,
    w_down,
    cotangent,
):
    if can_gather(axes, w_qkv, w_out, w_up, w_down):
        hidden, qkv, full_qkv, full_out, full_up, part_down = gather_embed(
            axes,
            size_group,
            tokens,
            pos_index,
            pos_table,
            prompts,
            norm_gains,
            w_qkv,
            w_out,
            w_up,
            w_down,
        )
        mixed, totals = attend(size_group, qkv)
        outputs, middle_grad, mixed_grad = gather_feed(
            axes,
            size_group,
            hidden,
            mixed,
            cotangent,
            norm_gains,
            full_out,
            full_up,
            w_down,
            part_down,
        )
    else:
        full_qkv = lax.all_gather(w_qkv, "wide", axis=0, tiled=True)
        full_out = lax.all_gather(w_out, "wide", axis=0, tiled=True)
        full_up = lax.all_gather(w_up, "wide", axis=0, tiled=True)
        full_down = lax.all_gather(w_down, "wide", axis=0, tiled=True)
        hidden, qkv = embed(size_group, tokens, pos_index, pos_table, prompts, norm_gains, full_qkv)
        mixed, totals = attend(size_group, qkv)
        outputs, middle_grad, mixed_grad = feed(
            size_group, hidden, mixed, cotangent, norm_gains, full_out, full_up, full_down
        )
    dq, dk, dv, *sums, outputs = attend_back(
        size_group, qkv, mixed_grad, mixed, totals, middle_grad, outputs
    )
    input_grad, prompt_grad, penalty = finish(
        axes, size_group, prompts, norm_gains, sums, hidden, middle_grad, dq, dk, dv, full_qkv
    )
    return (outputs, input_grad, prompt_grad, penalty)


def solution(mesh):
    return jax.shard_map(
        functools.partial(shards, dict(mesh.shape)),
        mesh=mesh,
        in_specs=(
            P(("dp", "wide"), None),
            P(("dp", "wide"), None),
            P(("dp", "wide")),
            P(),
            P(),
            P(),
            P("wide", None),
            P("wide", None),
            P("wide", None),
            P("wide", None),
            P(("dp", "wide"), None),
        ),
        out_specs=(P(("dp", "wide"), None), P(("dp", "wide"), None), P(), P()),
        check_vma=False,
    )
```

profile of v0, /device:TPU:0, one launch (start us, length us, event | category | flops | bytes accessed | tf_op | source)
XLA Modules:
  0.0 157.6 jit_solution(2716621957990858805)
XLA Ops:
  0.6 50.9 %gather_embed.1 = (f32[1152,768]{1,0:T(8,128)}, bf16[1152,2304]{1,0:T(8,128)(2,1)}, bf16[768,2304]{1,0:T(8,128)(2,1)}, bf16[768,768]{1,0:T(8,128)(2,1)}, bf16[76...) custom-call(s32[7]{0:T(128)} %groups.9, bf16[197,768]{1,0:T(8,128)(2,1)} %pos_table.1, f32[50,768]{1,0:T(8,128)} %prompts.3, ...), custom_call_target="tpu_custom_call" | custom-call | tf_op jit(solution)/shard_map/gather_embed/pallas_call | solution.py:523
  51.6 6.6 %attend.1 = (bf16[1152,768]{1,0:T(8,128)(2,1)}, f32[2,42,1,640]{3,2,1,0:T(1,128)}) custom-call(s32[7]{0:T(128)} %groups.9, bf16[1152,2304]{1,0:T(8,128)(2,1)} %get-tuple-element.26.q_ref.k_ref.v_ref, bf16[1152,2304]{1,0:T(8,128)(2,1)} %get-tuple-element.26.q_ref.k_ref.v_ref, bf16[1152,2304]{1,0:T(8,128)(2,1)} %get-tuple-element.26.q_ref.k_ref.v_ref), custom_call_target="tpu_custom_call" | custom-call | tf_op jit(solution)/shard_map/attend/pallas_call | solution.py:693
  58.2 50.5 %gather_feed.1 = (bf16[1152,768]{1,0:T(8,128)(2,1)}, f32[1152,768]{1,0:T(8,128)}, bf16[1152,768]{1,0:T(8,128)(2,1)}) custom-call(s32[7]{0:T(128)} %groups.9, f32[2,768]{1,0:T(2,128)} %gains.5, f32[1152,768]{1,0:T(8,128)} %get-tuple-element.27.hidden_in, bf16[1152,768]{1,0:T(8,128)(2,1)} %get-tuple-element.28.mixed_in.mixed_ref, ...), custom_call_target="tpu_custom_call" | custom-call | tf_op jit(solution)/shard_map/gather_feed/pallas_call | solution.py:1075
  108.7 10.9 %attend_back.1 = (bf16[1152,768]{1,0:T(8,128)(2,1)}, bf16[1152,768]{1,0:T(8,128)(2,1)}, bf16[1152,768]{1,0:T(8,128)(2,1)}, f32[64,768]{1,0:T(8,128)}, f32[64,768...) custom-call(s32[7]{0:T(128)} %groups.9, ...), custom_call_target="tpu_custom_call" | custom-call | tf_op jit(solution)/shard_map/attend_back/pallas_call | solution.py:809
  119.5 32.8 %finish.1 = (bf16[1152,768]{1,0:T(8,128)(2,1)}, f32[50,768]{1,0:T(8,128)}, f32[1,1]{1,0:T(1,128)}) custom-call(s32[7]{0:T(128)} %groups.9, f32[50,768]{1,0:T(8,128)} %prompts.3, f32[2,768]{1,0:T(2,128)} %gains.5, f32[64,768]{1,0:T(8,128)} %get-tuple-element.37.dq_sum, f32[64,768]{1,0:T(8,128)} %get-tuple-element.38.dk_sum, ...), custom_call_target="tpu_custom_call" | custom-call | tf_op jit(solution)/shard_map/finish/pallas_call | solution.py:1341
  152.3 0.0 copy-start
  152.3 2.8 %copy.18 = bf16[1152,768]{1,0:T(8,128)(2,1)} copy(bf16[1152,768]{1,0:T(8,128)(2,1)} %get-tuple-element.53) | data formatting | bytes 3538944
  155.2 0.0 copy-done
  155.2 0.7 copy.19
Async XLA Ops:
  152.3 2.8 %copy-start = (f32[50,768]{1,0:T(8,128)S(1)}, f32[50,768]{1,0:T(8,128)}, u32[]{:S(2)}) copy-start(f32[50,768]{1,0:T(8,128)} %get-tuple-element.54) | copy-start | bytes 460804
where the time goes:
time: 158 us
  Pallas kernels  152 us (96%)
  local copies, waits for them, and re-layouts  3.51 us (2%)
  between operations  2.42 us (2%)
    pallas_call x1, Pallas kernels, gather_embed(): pl.pallas_call(functools.partial(gather_embed_kernel, planes, size_group....  50.9 us
    pallas_call x1, Pallas kernels, gather_feed(): pl.pallas_call(functools.partial(gather_feed_kernel, planes, size_group.s...  50.5 us
    pallas_call x1, Pallas kernels, finish(): pl.pallas_call(functools.partial(finish_kernel, dp, wide, size_group.shap...  32.8 us
    pallas_call x1, Pallas kernels, attend_back(): pl.pallas_call(functools.partial(attend_back_kernel, slots), grid_spec=pl...  10.9 us
    pallas_call x1, Pallas kernels, attend(): pl.pallas_call(functools.partial(attend_kernel, slots), grid_spec=pltpu.P...  6.58 us
    unnamed x4, local copies, waits for them, and re-layouts  3.51 us

commit v1 on v0

--- a/solution.py
+++ b/solution.py
@@ -710,12 +710,46 @@
     )(size_group, qkv, qkv, qkv)
 
 
-def attend_back_kernel(slots, groups, q_ref, k_ref, v_ref, grad_ref, mixed_ref, total_ref, *refs):
+def back_through_qkv(q, k, v, w_qkv):
+    width = q.shape[1]
+    return (
+        dot(q, w_qkv[:, :width], NT)
+        + dot(k, w_qkv[:, width : 2 * width], NT)
+        + dot(v, w_qkv[:, 2 * width :], NT)
+    )
+
+
+def attend_back_kernel(
+    slots,
+    groups,
+    prompts,
+    gains,
+    w_qkv_in,
+    q_ref,
+    k_ref,
+    v_ref,
+    grad_ref,
+    mixed_ref,
+    total_ref,
+    *refs,
+):
     middles, refs = refs[:PAIRS], refs[PAIRS:]
-    passed_in, dq_ref, dk_ref, dv_ref, dq_sum, dk_sum, dv_sum, middle_sum, passed_out = refs
+    passed_in, dq_ref, dk_ref, dv_ref, prompt_terms, passed_out = refs[:6]
+    dq_sum, dk_sum, dv_sum, middle_sum, known, w_qkv, weight_in = refs[6:]
+    step = pl.program_id(0)
+    weight_load = pltpu.make_async_copy(w_qkv_in, w_qkv, weight_in)
+
+    @pl.when(step == 0)
+    def _():
+        weight_load.start()
+        for ref in (dq_sum, dk_sum, dv_sum, middle_sum, known):
+            ref[...] = jnp.zeros_like(ref)
+        known[: prompts.shape[0]] = prompts[...]
+
     passed_out[...] = passed_in[...]
-    for ref in (dq_sum, dk_sum, dv_sum, middle_sum):
-        ref[...] = jnp.zeros_like(ref)
+
+    def sum_columns(pair):
+        return pl.ds(pl.multiple_of(step * HEAD_COLS + LANES * pair, LANES), LANES)
 
     def image(size, start, length, slot):
         all_rows = dq_ref.shape[0]
@@ -737,8 +771,7 @@
             row = lax.broadcasted_iota(jnp.int32, (SLOT_ROWS, count), 1)
             chosen = (row == slot_row + before + 1) & (slot_row < PROMPTS)
             chosen = jnp.where(chosen, 1.0, 0.0).astype(BF)
-            columns = slice(LANES * pair, LANES * (pair + 1))
-            total[:, columns] += dot(chosen, values[:count].astype(BF))
+            total[:, sum_columns(pair)] += dot(chosen, values[:count].astype(BF))
 
         for chunk, count in chunks:
             rows = pl.ds(pl.multiple_of(first + chunk, 8), count)
@@ -793,13 +826,26 @@
             put(dv_ref, key_rows, pair, dv[pair], key_inside)
             add_prompts(dk_sum, pair, dk[pair] * SCALE, key_shift)
             add_prompts(dv_sum, pair, dv[pair], key_shift)
-            columns = slice(LANES * pair, LANES * (pair + 1))
-            middle_sum[:, columns] += middles[pair][pl.ds(start + 1, SLOT_ROWS), :]
+            middle_sum[:, sum_columns(pair)] += middles[pair][pl.ds(start + 1, SLOT_ROWS), :]
 
     each_image(groups, slots, image)
 
-
-def attend_back(size_group, qkv, mixed_grad, mixed, totals, middle_grad, passed):
+    @pl.when(step == pl.num_programs(0) - 1)
+    def _():
+        weight_load.wait()
+        pieces = []
+        for ref in (dq_sum, dk_sum, dv_sum):
+            high = ref[...].astype(BF)
+            pieces.append(jnp.concatenate([high, (ref[...] - high.astype(F32)).astype(BF)], 0))
+        terms = back_through_qkv(*pieces, w_qkv)
+        normed_grad = terms[:SLOT_ROWS] + terms[SLOT_ROWS:]
+        normal, rstd = norm_parts(known[...])
+        prompt_terms[...] = middle_sum[...] + norm_back(normal, rstd, gains[0:1], normed_grad)
+
+
+def attend_back(
+    size_group, prompts, gains, w_qkv, qkv, mixed_grad, mixed, totals, middle_grad, passed
+):
     rows = qkv.shape[0]
     width = qkv.shape[1] // 3
     steps = width // HEAD_COLS
@@ -812,6 +858,9 @@
             num_scalar_prefetch=1,
             grid=(steps,),
             in_specs=[
+                pl.BlockSpec(prompts.shape, lambda i, g: (0, 0)),
+                pl.BlockSpec(gains.shape, lambda i, g: (0, 0)),
+                pl.BlockSpec(memory_space=pltpu.HBM),
                 block(0),
                 block(1),
                 block(2),
@@ -822,16 +871,22 @@
             + [middle(pair) for pair in range(PAIRS)]
             + [block(0)],
             out_specs=[block(0)] * 3
-            + [pl.BlockSpec((SLOT_ROWS, HEAD_COLS), lambda i, g: (0, i))] * 4
-            + [block(0)],
+            + [pl.BlockSpec((SLOT_ROWS, width), lambda i, g: (0, 0)), block(0)],
+            scratch_shapes=[pltpu.VMEM((SLOT_ROWS, width), F32)] * 5
+            + [pltpu.VMEM(w_qkv.shape, BF), pltpu.SemaphoreType.DMA],
         ),
         out_shape=[jax.ShapeDtypeStruct((rows, width), BF)] * 3
-        + [jax.ShapeDtypeStruct((SLOT_ROWS, width), F32)] * 4
-        + [jax.ShapeDtypeStruct((rows, width), BF)],
+        + [
+            jax.ShapeDtypeStruct((SLOT_ROWS, width), F32),
+            jax.ShapeDtypeStruct((rows, width), BF),
+        ],
         compiler_params=pltpu.CompilerParams(vmem_limit_bytes=VMEM_LIMIT),
         name="attend_back",
     )(
         size_group,
+        prompts,
+        gains,
+        w_qkv,
         qkv,
         qkv,
         qkv,
@@ -995,7 +1050,6 @@
         down.exchange(down.nearest(k))
     down.give(down.plane)
     out_load.wait()
-    up_load.wait()
     gain = gains[1:2]
 
     def pump(step):
@@ -1016,6 +1070,7 @@
         middle[part, :] = value
         normal, _ = norm_parts(value)
         second = (normal * gain).astype(BF)
+        pl.when(index == 0)(up_load.wait)
         for first in range(0, inner_width, chunk):
             columns = slice(first, first + chunk)
             inner = dot(second, w_up[:, columns])
@@ -1073,7 +1128,7 @@
     dma = pltpu.SemaphoreType.DMA
     count = Gather.semaphores(planes)
     return pl.pallas_call(
-        functools.partial(gather_feed_kernel, planes, size_group.shape[0], 512),
+        functools.partial(gather_feed_kernel, planes, size_group.shape[0], 768),
         in_specs=[
             pl.BlockSpec(memory_space=pltpu.SMEM),
             pl.BlockSpec(memory_space=pltpu.VMEM),
@@ -1111,7 +1166,7 @@
     def __init__(self, dp, wide, mine, near, far, result, sems):
         self.members = 2 * dp
         self.planes = wide // 2
-        self.rows = mine.shape[0] // self.members
+        self.rows = mine.shape[1]
         self.d = lax.axis_index("dp")
         w = lax.axis_index("wide")
         self.plane = w // 2
@@ -1149,7 +1204,7 @@
     def first(self, step):
         other, device = self.peer(step)
         return self.copy(
-            self.part(self.mine, other),
+            self.mine.at[other],
             self.near.at[step],
             self.send.at[0, step],
             self.near_in.at[step],
@@ -1169,15 +1224,16 @@
     def start_first(self):
         for step in range(1, self.members):
             self.first(step).start()
-        self.near[0] = self.part(self.mine, self.member)[...]
+        self.near[0] = self.mine[self.member]
 
     def start_second(self):
         for step in range(1, self.members):
             self.first(step).wait_recv()
         total = jnp.zeros(self.near.shape[1:], F32)
         for index in range(self.members):
-            total = total + self.near[lax.rem(self.member - index + self.members, self.members)]
-        self.far[self.plane] = total
+            place = lax.rem(self.member - index + self.members, self.members)
+            total = total + self.near[place].astype(F32)
+        self.far[self.plane] = total.astype(BF)
         for step in range(1, self.planes):
             self.second(step).start()
 
@@ -1186,7 +1242,7 @@
             self.second(step).wait_recv()
         total = jnp.zeros(self.near.shape[1:], F32)
         for index in range(self.planes):
-            total = total + self.far[index]
+            total = total + self.far[index].astype(F32)
         self.part(self.result, self.member)[...] = total
         for step in range(1, self.members):
             self.third(step).start()
@@ -1208,10 +1264,7 @@
     groups,
     prompts,
     gains,
-    dq_sum,
-    dk_sum,
-    dv_sum,
-    middle_sum,
+    prompt_terms,
     hidden_in,
     middle_grad_in,
     dq_in,
@@ -1228,7 +1281,6 @@
     dv,
     w_qkv,
     input_grad,
-    known,
     mine,
     near,
     far,
@@ -1270,33 +1322,17 @@
         for copy in loads(index):
             copy.start()
 
-    def back(q, k, v):
-        return (
-            dot(q, w_qkv[:, :width], NT)
-            + dot(k, w_qkv[:, width : 2 * width], NT)
-            + dot(v, w_qkv[:, 2 * width :], NT)
-        )
-
-    known[...] = jnp.zeros_like(known)
-    known[: prompts.shape[0]] = prompts[...]
-    pieces = []
-    for ref in (dq_sum, dk_sum, dv_sum):
-        rest = ref[...]
-        terms = []
-        for _ in range(2):
-            terms.append(rest.astype(BF))
-            rest = rest - terms[-1].astype(F32)
-        pieces.append(jnp.concatenate(terms, 0))
-    weight_load.wait()
-    terms = back(*pieces)
-    normed_grad = terms[:SLOT_ROWS] + terms[SLOT_ROWS:]
-    normal, rstd = norm_parts(known[...])
-    local = middle_sum[...] + norm_back(normal, rstd, gains[0:1], normed_grad)
     slot_row = lax.broadcasted_iota(jnp.int32, (SLOT_ROWS, 1), 0)
-    count = total_length(groups, slots).astype(F32)
-    mine[...] = jnp.where(slot_row < PROMPTS, local, jnp.where(slot_row == PROMPTS, count, 0.0))
+    shifted = total_length(groups, slots) + lax.broadcasted_iota(jnp.int32, (1, width), 1)
+    shares = jnp.zeros((1, width), F32)
+    for least in range(width, hidden.shape[0] + width, width):
+        shares = shares + jnp.where(shifted >= least, 1.0, 0.0)
+    terms = jnp.where(slot_row < PROMPTS, prompt_terms[...], jnp.where(slot_row == PROMPTS, shares, 0.0))
+    for member in range(mine.shape[0]):
+        mine[member] = terms[member * mine.shape[1] : (member + 1) * mine.shape[1]].astype(BF)
     pl.semaphore_wait(barrier, greeted)
     shared.start_first()
+    weight_load.wait()
 
     def store(index):
         part = tile_rows(index)
@@ -1309,7 +1345,7 @@
             copy.wait()
         part = tile_rows(index)
         normal, rstd = norm_parts(hidden[part, :])
-        normed_grad = back(dq[part, :], dk[part, :], dv[part, :])
+        normed_grad = back_through_qkv(dq[part, :], dk[part, :], dv[part, :], w_qkv)
         hidden_grad = middle_grad[part, :] + norm_back(normal, rstd, gains[0:1], normed_grad)
         prompt_slot, live = row_places(groups, slots, index * tile, tile)
         input_grad[part, :] = jnp.where(live & (prompt_slot < 0), hidden_grad, 0.0).astype(BF)
@@ -1322,15 +1358,15 @@
     shared.end()
     given = prompts[...]
     size = given.shape[0] * given.shape[1]
-    count = result[PROMPTS : PROMPTS + 1]
+    count = jnp.sum(result[PROMPTS : PROMPTS + 1], axis=1, keepdims=True)
     prompt_grad[...] = result[:PROMPTS] + (2.0 * PENALTY_RATE / size) * count * given
     square = jnp.sum(jnp.sum(given * given, axis=1, keepdims=True), axis=0, keepdims=True)
-    penalty[...] = PENALTY_RATE * count[:, :1] * (square / size)
+    penalty[...] = PENALTY_RATE * count * (square / size)
     for index in range(tiles):
         store(index).wait()
 
 
-def finish(axes, size_group, prompts, gains, sums, hidden, middle_grad, dq, dk, dv, w_qkv):
+def finish(axes, size_group, prompts, gains, terms, hidden, middle_grad, dq, dk, dv, w_qkv):
     rows, width = hidden.shape
     dp, wide = axes["dp"], axes["wide"]
     members, planes = 2 * dp, wide // 2
@@ -1340,7 +1376,7 @@
     hbm = pl.BlockSpec(memory_space=pltpu.HBM)
     input_grad, prompt_grad, penalty = pl.pallas_call(
         functools.partial(finish_kernel, dp, wide, size_group.shape[0]),
-        in_specs=[pl.BlockSpec(memory_space=pltpu.SMEM)] + [vmem] * 6 + [hbm] * 6,
+        in_specs=[pl.BlockSpec(memory_space=pltpu.SMEM)] + [vmem] * 3 + [hbm] * 6,
         out_specs=[hbm, vmem, vmem],
         out_shape=[
             jax.ShapeDtypeStruct((rows, width), BF),
@@ -1355,10 +1391,9 @@
             pltpu.VMEM((rows, width), BF),
             pltpu.VMEM(w_qkv.shape, BF),
             pltpu.VMEM((rows, width), BF),
-            pltpu.VMEM((SLOT_ROWS, width), F32),
-            pltpu.VMEM((SLOT_ROWS, width), F32),
-            pltpu.VMEM((members, SLOT_ROWS // members, width), F32),
-            pltpu.VMEM((planes, SLOT_ROWS // members, width), F32),
+            pltpu.VMEM((members, SLOT_ROWS // members, width), BF),
+            pltpu.VMEM((members, SLOT_ROWS // members, width), BF),
+            pltpu.VMEM((planes, SLOT_ROWS // members, width), BF),
             pltpu.VMEM((SLOT_ROWS, width), F32),
             dma((3, max(members, planes))),
             dma((members,)),
@@ -1372,7 +1407,7 @@
             collective_id=1, has_side_effects=True, vmem_limit_bytes=VMEM_LIMIT
         ),
         name="finish",
-    )(size_group, prompts, gains, *sums, hidden, middle_grad, dq, dk, dv, w_qkv)
+    )(size_group, prompts, gains, terms, hidden, middle_grad, dq, dk, dv, w_qkv)
     return input_grad, prompt_grad, penalty[0, 0]
 
 
@@ -1427,11 +1462,20 @@
         outputs, middle_grad, mixed_grad = feed(
             size_group, hidden, mixed, cotangent, norm_gains, full_out, full_up, full_down
         )
-    dq, dk, dv, *sums, outputs = attend_back(
-        size_group, qkv, mixed_grad, mixed, totals, middle_grad, outputs
+    dq, dk, dv, terms, outputs = attend_back(
+        size_group,
+        prompts,
+        norm_gains,
+        full_qkv,
+        qkv,
+        mixed_grad,
+        mixed,
+        totals,
+        middle_grad,
+        outputs,
     )
     input_grad, prompt_grad, penalty = finish(
-        axes, size_group, prompts, norm_gains, sums, hidden, middle_grad, dq, dk, dv, full_qkv
+        axes, size_group, prompts, norm_gains, terms, hidden, middle_grad, dq, dk, dv, full_qkv
     )
     return (outputs, input_grad, prompt_grad, penalty)
 

time: 158 us -> 157 us (level)
  no operation moved by 1% of the time
where the time goes in v1:
time: 157 us
  Pallas kernels  151 us (96%)
  local copies, waits for them, and re-layouts  3.51 us (2%)
  between operations  2.43 us (2%)
    pallas_call x1, Pallas kernels, gather_feed(): pl.pallas_call(functools.partial(gather_feed_kernel, planes, size_group.s...  51.5 us
    pallas_call x1, Pallas kernels, gather_embed(): pl.pallas_call(functools.partial(gather_embed_kernel, planes, size_group....  50.9 us
    pallas_call x1, Pallas kernels, finish(): pl.pallas_call(functools.partial(finish_kernel, dp, wide, size_group.shap...  32.8 us
    pallas_call x1, Pallas kernels, attend_back(): pl.pallas_call(functools.partial(attend_back_kernel, slots), grid_spec=pl...  10.8 us
    pallas_call x1, Pallas kernels, attend(): pl.pallas_call(functools.partial(attend_kernel, slots), grid_spec=pltpu.P...  5.22 us
    unnamed x4, local copies, waits for them, and re-layouts  3.51 us

profile of v1, /device:TPU:0, one launch (start us, length us, event | category | flops | bytes accessed | tf_op | source)
XLA Modules:
  0.0 157.2 jit_solution(11047453187483926497)
XLA Ops:
  0.6 50.9 %gather_embed.1 = (f32[1152,768]{1,0:T(8,128)}, bf16[1152,2304]{1,0:T(8,128)(2,1)}, bf16[768,2304]{1,0:T(8,128)(2,1)}, bf16[768,768]{1,0:T(8,128)(2,1)}, bf16[76...) custom-call(s32[7]{0:T(128)} %groups.9, bf16[197,768]{1,0:T(8,128)(2,1)} %pos_table.1, f32[50,768]{1,0:T(8,128)} %prompts.5, ...), custom_call_target="tpu_custom_call" | custom-call | tf_op jit(solution)/shard_map/gather_embed/pallas_call | solution.py:523
  51.6 5.2 %attend.1 = (bf16[1152,768]{1,0:T(8,128)(2,1)}, f32[2,42,1,640]{3,2,1,0:T(1,128)}) custom-call(s32[7]{0:T(128)} %groups.9, bf16[1152,2304]{1,0:T(8,128)(2,1)} %get-tuple-element.24.q_ref.k_ref.v_ref, bf16[1152,2304]{1,0:T(8,128)(2,1)} %get-tuple-element.24.q_ref.k_ref.v_ref, bf16[1152,2304]{1,0:T(8,128)(2,1)} %get-tuple-element.24.q_ref.k_ref.v_ref), custom_call_target="tpu_custom_call" | custom-call | tf_op jit(solution)/shard_map/attend/pallas_call | solution.py:693
  56.8 51.5 %gather_feed.1 = (bf16[1152,768]{1,0:T(8,128)(2,1)}, f32[1152,768]{1,0:T(8,128)}, bf16[1152,768]{1,0:T(8,128)(2,1)}) custom-call(s32[7]{0:T(128)} %groups.9, f32[2,768]{1,0:T(2,128)} %gains.7, f32[1152,768]{1,0:T(8,128)} %get-tuple-element.25.hidden_in, bf16[1152,768]{1,0:T(8,128)(2,1)} %get-tuple-element.26.mixed_in.mixed_ref, ...), custom_call_target="tpu_custom_call" | custom-call | tf_op jit(solution)/shard_map/gather_feed/pallas_call | solution.py:1130
  108.3 10.8 %attend_back.1 = (bf16[1152,768]{1,0:T(8,128)(2,1)}, bf16[1152,768]{1,0:T(8,128)(2,1)}, bf16[1152,768]{1,0:T(8,128)(2,1)}, f32[64,768]{1,0:T(8,128)}, bf16[1152,768]{1,0:T(8,128)(2,1)}) custom-call(s32[7]{0:T(128)} %groups.9, f32[50,768]{1,0:T(8,128)} %prompts.5, f32[2,768]{1,0:T(2,128)} %gains.7, bf16[768,2304]{1,0:T(8,128)(2,1)} %get-tuple-element.23.w_qkv_in, ...), custom_call_target="tpu_custom_call" | custom-call | tf_op jit(solution)/shard_map/attend_back/pallas_call | solution.py:855
  119.1 32.8 %finish.1 = (bf16[1152,768]{1,0:T(8,128)(2,1)}, f32[50,768]{1,0:T(8,128)}, f32[1,1]{1,0:T(1,128)}) custom-call(s32[7]{0:T(128)} %groups.9, f32[50,768]{1,0:T(8,128)} %prompts.5, f32[2,768]{1,0:T(2,128)} %gains.7, f32[64,768]{1,0:T(8,128)} %get-tuple-element.35.prompt_terms, f32[1152,768]{1,0:T(8,128)} %get-tuple-element.25.hidden_in, ...), custom_call_target="tpu_custom_call" | custom-call | tf_op jit(solution)/shard_map/finish/pallas_call | solution.py:1377
  151.9 0.0 copy-start
  151.9 2.8 %copy.18 = bf16[1152,768]{1,0:T(8,128)(2,1)} copy(bf16[1152,768]{1,0:T(8,128)(2,1)} %get-tuple-element.47) | data formatting | bytes 3538944
  154.7 0.0 copy-done
  154.7 0.7 copy.19
Async XLA Ops:
  151.9 2.8 %copy-start = (f32[50,768]{1,0:T(8,128)S(1)}, f32[50,768]{1,0:T(8,128)}, u32[]{:S(2)}) copy-start(f32[50,768]{1,0:T(8,128)} %get-tuple-element.48) | copy-start | bytes 460804

commit v2 on v1

--- a/solution.py
+++ b/solution.py
@@ -658,11 +658,17 @@
             rows = pair if len(block) == 2 else head_rows(pair, block[0])
             return jnp.concatenate([rows, ones], 0)
 
-        for chunk, count in chunks:
+        def scores_of(chunk, count):
             rows = pl.ds(pl.multiple_of(first + chunk, 8), count)
             query = take(q_ref, rows)
             blocks = blocks_of(count)
-            scores = [keys.scores(block, query) for block in blocks]
+            return rows, blocks, [keys.scores(block, query) for block in blocks]
+
+        ahead = scores_of(*chunks[0])
+        for number, (chunk, count) in enumerate(chunks):
+            rows, blocks, scores = ahead
+            if number + 1 < len(chunks):
+                ahead = scores_of(*chunks[number + 1])
             peaks = [jnp.max(s, axis=0, keepdims=True) * SCORE for s in scores]
             powers = [jnp.exp2(s * SCORE - m).astype(BF) for s, m in zip(scores, peaks)]
             mixed = [dot(values_of(block), e) for block, e in zip(blocks, powers)]
@@ -671,9 +677,9 @@
                 depth = HEAD_DIM * len(block)
                 sums = value[depth : depth + 1]
                 total = peak + jnp.log2(sums)
-                for number, head in enumerate(block):
+                for place, head in enumerate(block):
                     total_ref[0, GROUP_HEADS * slot + head, :, chunk : chunk + count] = total[
-                        :, number * count : (number + 1) * count
+                        :, place * count : (place + 1) * count
                     ]
                 value = value[:depth] / sums
                 parts += [value] if len(block) == 1 else own_quarters(value)
@@ -1271,7 +1277,7 @@
     dk_in,
     dv_in,
     w_qkv_in,
-    input_grad_out,
+    input_grad,
     prompt_grad,
     penalty,
     hidden,
@@ -1280,7 +1286,6 @@
     dk,
     dv,
     w_qkv,
-    input_grad,
     mine,
     near,
     far,
@@ -1291,7 +1296,6 @@
     last_in,
     weight_in,
     rows_in,
-    rows_out,
 ):
     shared = Shared(dp, wide, mine, near, far, result, (send, near_in, far_in, last_in))
     barrier, greeted = shared.greet()
@@ -1334,12 +1338,6 @@
     shared.start_first()
     weight_load.wait()
 
-    def store(index):
-        part = tile_rows(index)
-        return pltpu.make_async_copy(
-            input_grad.at[part], input_grad_out.at[part], rows_out.at[index]
-        )
-
     def row_tile(index, carry):
         for copy in loads(index):
             copy.wait()
@@ -1349,7 +1347,6 @@
         hidden_grad = middle_grad[part, :] + norm_back(normal, rstd, gains[0:1], normed_grad)
         prompt_slot, live = row_places(groups, slots, index * tile, tile)
         input_grad[part, :] = jnp.where(live & (prompt_slot < 0), hidden_grad, 0.0).astype(BF)
-        store(index).start()
         pl.when(index == 0)(shared.start_second)
         pl.when(index == 1)(shared.start_third)
         return carry
@@ -1362,8 +1359,6 @@
     prompt_grad[...] = result[:PROMPTS] + (2.0 * PENALTY_RATE / size) * count * given
     square = jnp.sum(jnp.sum(given * given, axis=1, keepdims=True), axis=0, keepdims=True)
     penalty[...] = PENALTY_RATE * count * (square / size)
-    for index in range(tiles):
-        store(index).wait()
 
 
 def finish(axes, size_group, prompts, gains, terms, hidden, middle_grad, dq, dk, dv, w_qkv):
@@ -1377,10 +1372,10 @@
     input_grad, prompt_grad, penalty = pl.pallas_call(
         functools.partial(finish_kernel, dp, wide, size_group.shape[0]),
         in_specs=[pl.BlockSpec(memory_space=pltpu.SMEM)] + [vmem] * 3 + [hbm] * 6,
-        out_specs=[hbm, vmem, vmem],
+        out_specs=[vmem, vmem, vmem],
         out_shape=[
-            jax.ShapeDtypeStruct((rows, width), BF),
-            jax.ShapeDtypeStruct(prompts.shape, F32),
+            pltpu.VMEM((rows, width), BF),
+            pltpu.VMEM(prompts.shape, F32),
             jax.ShapeDtypeStruct((1, 1), F32),
         ],
         scratch_shapes=[
@@ -1390,7 +1385,6 @@
             pltpu.VMEM((rows, width), BF),
             pltpu.VMEM((rows, width), BF),
             pltpu.VMEM(w_qkv.shape, BF),
-            pltpu.VMEM((rows, width), BF),
             pltpu.VMEM((members, SLOT_ROWS // members, width), BF),
             pltpu.VMEM((members, SLOT_ROWS // members, width), BF),
             pltpu.VMEM((planes, SLOT_ROWS // members, width), BF),
@@ -1401,10 +1395,9 @@
             dma((members,)),
             dma,
             dma((tiles, 5)),
-            dma((tiles,)),
         ],
         compiler_params=pltpu.CompilerParams(
-            collective_id=1, has_side_effects=True, vmem_limit_bytes=VMEM_LIMIT
+            collective_id=1, has_side_effects=True, vmem_limit_bytes=VMEM_LIMIT - (2 << 20)
         ),
         name="finish",
     )(size_group, prompts, gains, terms, hidden, middle_grad, dq, dk, dv, w_qkv)

time: 157 us -> 154 us (0.981)
  local copies, waits for them, and re-layouts: 3.51 us -> 1.88 us
    unnamed x4 -> x2, local copies, waits for them, and re-layouts: 3.51 us -> 1.88 us
where the time goes in v2:
time: 154 us
  Pallas kernels  150 us (97%)
  between operations  2.43 us (2%)
  local copies, waits for them, and re-layouts  1.88 us (1%)
    pallas_call x1, Pallas kernels, gather_embed(): pl.pallas_call(functools.partial(gather_embed_kernel, planes, size_group....  50.9 us
    pallas_call x1, Pallas kernels, gather_feed(): pl.pallas_call(functools.partial(gather_feed_kernel, planes, size_group.s...  50.4 us
    pallas_call x1, Pallas kernels, finish(): pl.pallas_call(functools.partial(finish_kernel, dp, wide, size_group.shap...  32.2 us
    pallas_call x1, Pallas kernels, attend_back(): pl.pallas_call(functools.partial(attend_back_kernel, slots), grid_spec=pl...  10.8 us
    pallas_call x1, Pallas kernels, attend(): pl.pallas_call(functools.partial(attend_kernel, slots), grid_spec=pltpu.P...  5.22 us

profile of v2, /device:TPU:0, one launch (start us, length us, event | category | flops | bytes accessed | tf_op | source)
XLA Modules:
  0.0 153.8 jit_solution(18223434293546370837)
XLA Ops:
  0.6 50.9 %gather_embed.1 = (f32[1152,768]{1,0:T(8,128)}, bf16[1152,2304]{1,0:T(8,128)(2,1)}, bf16[768,2304]{1,0:T(8,128)(2,1)}, bf16[768,768]{1,0:T(8,128)(2,1)}, bf16[76...) custom-call(s32[7]{0:T(128)} %groups.9, bf16[197,768]{1,0:T(8,128)(2,1)} %pos_table.1, f32[50,768]{1,0:T(8,128)} %prompts.5, ...), custom_call_target="tpu_custom_call" | custom-call | tf_op jit(solution)/shard_map/gather_embed/pallas_call | solution.py:523
  51.6 5.2 %attend.1 = (bf16[1152,768]{1,0:T(8,128)(2,1)}, f32[2,42,1,640]{3,2,1,0:T(1,128)}) custom-call(s32[7]{0:T(128)} %groups.9, bf16[1152,2304]{1,0:T(8,128)(2,1)} %get-tuple-element.24.q_ref.k_ref.v_ref, bf16[1152,2304]{1,0:T(8,128)(2,1)} %get-tuple-element.24.q_ref.k_ref.v_ref, bf16[1152,2304]{1,0:T(8,128)(2,1)} %get-tuple-element.24.q_ref.k_ref.v_ref), custom_call_target="tpu_custom_call" | custom-call | tf_op jit(solution)/shard_map/attend/pallas_call | solution.py:699
  56.8 50.4 %gather_feed.1 = (bf16[1152,768]{1,0:T(8,128)(2,1)}, f32[1152,768]{1,0:T(8,128)}, bf16[1152,768]{1,0:T(8,128)(2,1)}) custom-call(s32[7]{0:T(128)} %groups.9, f32[2,768]{1,0:T(2,128)} %gains.7, f32[1152,768]{1,0:T(8,128)} %get-tuple-element.25.hidden_in, bf16[1152,768]{1,0:T(8,128)(2,1)} %get-tuple-element.26.mixed_in.mixed_ref, ...), custom_call_target="tpu_custom_call" | custom-call | tf_op jit(solution)/shard_map/gather_feed/pallas_call | solution.py:1136
  107.2 10.8 %attend_back.1 = (bf16[1152,768]{1,0:T(8,128)(2,1)}, bf16[1152,768]{1,0:T(8,128)(2,1)}, bf16[1152,768]{1,0:T(8,128)(2,1)}, f32[64,768]{1,0:T(8,128)}, bf16[1152,768]{1,0:T(8,128)(2,1)}) custom-call(s32[7]{0:T(128)} %groups.9, f32[50,768]{1,0:T(8,128)} %prompts.5, f32[2,768]{1,0:T(2,128)} %gains.7, bf16[768,2304]{1,0:T(8,128)(2,1)} %get-tuple-element.23.w_qkv_in, ...), custom_call_target="tpu_custom_call" | custom-call | tf_op jit(solution)/shard_map/attend_back/pallas_call | solution.py:861
  118.0 32.2 %finish.1 = (bf16[1152,768]{1,0:T(8,128)(2,1)S(1)}, f32[50,768]{1,0:T(8,128)S(1)}, f32[1,1]{1,0:T(1,128)}) custom-call(s32[7]{0:T(128)} %groups.9, f32[50,768]{1,0:T(8,128)} %prompts.5, f32[2,768]{1,0:T(2,128)} %gains.7, f32[64,768]{1,0:T(8,128)} %get-tuple-element.35.prompt_terms, f32[1152,768]{1,0:T(8,128)} %get-tuple-element.25.hidden_in, ...), custom_call_target="tpu_custom_call" | custom-call | tf_op jit(solution)/shard_map/finish/pallas_call | solution.py:1372
  150.2 1.2 copy.18
  151.4 0.7 copy.19
